TPU v7x, 32 devices: a whole 2x2x4 slice. The times are simulated.
32 devices in a mesh: blk: 8 (over z, y), rep: 4 (over x, core).
Axes of the slice: x: 2, y: 2, z: 4, core: 2. Of those that a mesh axis runs over, the one named last changes fastest.
Arguments:
- point_xyz: float32 [3, 16384], P(None, ('blk', 'rep')), may hold values from -6 to 6
- point_attrs: float32 [5, 16384], P(None, ('blk', 'rep')), may hold values from -6 to 6
- scan_yaw: float32 [32], P(('blk', 'rep')), may hold values from -3.140625 to 3.140625
- scan_jitter: float32 [32, 3], P(('blk', 'rep')), may hold values from -0.5 to 0.5
- slot_counts: int32 [32, 8], P(('blk', 'rep')), may hold values from 0 to 64, as said below
- voxel_ids: int32 [16384], P(('blk', 'rep')), may hold values from 0 to 511
- point_weight: float32 [8, 96], replicated, may hold values from -2 to 2
- point_bias: float32 [96], replicated, may hold values from -3 to 3
- conv_one: bfloat16 [2592, 96], replicated, may hold values from -0.1875 to 0.1875
- conv_two: bfloat16 [2592, 128], replicated, may hold values from -0.1875 to 0.1875
- out_grad: bfloat16 [32, 64, 1024], P('rep', 'blk'), may hold values from -6 to 6
Outputs:
- block_out: bfloat16 [32, 64, 1024], P('rep', 'blk')
- attr_grad: float32 [5, 16384], P(None, ('blk', 'rep'))
- jitter_grad: float32 [32, 3], P(('blk', 'rep'))
- conv_one_grad: float32 [2592, 96], replicated
- conv_two_grad: float32 [2592, 128], replicated
Inputs may be any that keep to these rules, and one draw needn't show every extreme that they name: `slot_counts`: used slots out of 64; in every draw some voxel block receives 64 points from every scan of its slab. `voxel_ids`: voxel (x * 8 + y) * 8 + z inside the destination block; entries of unused slots are ignored.
All inputs are finite; a program needn't handle non-finite values.
Results may differ from a plain program's by a relative error of at most 0.006.
Values may be sent and summed in bfloat16 or wider, within the bound.
No kernel may reach another device: no remote copies, remote signals or barrier semaphores. Data moves between devices by JAX's collectives and lax.ppermute only.
A program may use at most 64 MiB of HBM per device.

v0:
```python
import jax
import jax.numpy as jnp
from jax import lax
from jax.sharding import PartitionSpec as P

SLOT_CAP = 64


def with_halo(cells, sides, width):
    for axis, dim in sides:
        count = lax.axis_size(axis)
        ends = count - 1
        head = lax.slice_in_dim(cells, 0, width, axis=dim)
        tail = lax.slice_in_dim(cells, cells.shape[dim] - width, cells.shape[dim], axis=dim)
        cells = jnp.concatenate(
            [
                lax.ppermute(tail, axis, [(i, (i + 1) % count) for i in range(ends)]),
                cells,
                lax.ppermute(head, axis, [((i + 1) % count, i) for i in range(ends)]),
            ],
            axis=dim,
        )
    return cells


def silu_slope(value):
    sigmoid_v = jax.nn.sigmoid(value)
    return sigmoid_v * (1.0 + value * (1.0 - sigmoid_v))


def point_layer(inputs, point_weight, point_bias):
    return (
        lax.dot_general(
            inputs, point_weight, (((0,), (0,)), ((), ())), precision=lax.Precision.HIGHEST
        )
        + point_bias
    )


def back_layer(grad_pre, point_weight):
    return lax.dot_general(
        point_weight, grad_pre, (((1,), (1,)), ((), ())), precision=lax.Precision.HIGHEST
    )


def with_faces(volume, channels):
    padded = with_halo(volume, (("blk", 1), ("rep", 0)), 1)
    shaped = padded.reshape(padded.shape[0], padded.shape[1], -1, channels)
    return jnp.pad(shaped, ((0, 0), (0, 0), (1, 1), (0, 0)))


def conv_apply(padded, weight, channels_in):
    kernel = weight.reshape(3, 3, 3, channels_in, weight.shape[1])
    result = lax.conv_general_dilated(
        padded[None],
        kernel,
        (1, 1, 1),
        "VALID",
        dimension_numbers=("NDHWC", "DHWIO", "NDHWC"),
        preferred_element_type=jnp.float32,
    )[0]
    return result.reshape(-1, weight.shape[1])


def kernel_grad(padded, partner, edge_len):
    channels_in = padded.shape[-1]
    channels_out = partner.shape[-1]
    source = jnp.transpose(padded, (3, 0, 1, 2))[..., None]
    target = partner.reshape(edge_len, edge_len, edge_len, 1, channels_out)
    result = lax.conv_general_dilated(
        source,
        target,
        (1, 1, 1),
        "VALID",
        dimension_numbers=("NDHWC", "DHWIO", "NDHWC"),
        preferred_element_type=jnp.float32,
    )
    return jnp.transpose(result, (1, 2, 3, 0, 4)).reshape(27 * channels_in, channels_out)


def flipped(weight, channels_in):
    taps = weight.reshape(3, 3, 3, channels_in, -1)[::-1, ::-1, ::-1]
    return jnp.swapaxes(taps, 3, 4).reshape(-1, channels_in)


def shards(
    point_xyz,
    point_attrs,
    scan_yaw,
    scan_jitter,
    slot_counts,
    voxel_ids,
    point_weight,
    point_bias,
    conv_one,
    conv_two,
    out_grad,
):
    owners = lax.axis_size("blk")
    edge_len = out_grad.shape[0]
    voxels = edge_len**3
    width_one = conv_one.shape[1]
    width_two = conv_two.shape[1]
    slot_index = lax.broadcasted_iota(jnp.int32, (owners, SLOT_CAP), 1)
    filled = slot_index < slot_counts[0][:, None]
    vox_sent = jnp.where(filled, voxel_ids.reshape(owners, SLOT_CAP), voxels)
    cos_yaw = jnp.cos(scan_yaw[0])
    sin_yaw = jnp.sin(scan_yaw[0])
    rotated_x = cos_yaw * point_xyz[0] - sin_yaw * point_xyz[1] + scan_jitter[0, 0]
    rotated_y = sin_yaw * point_xyz[0] + cos_yaw * point_xyz[1] + scan_jitter[0, 1]
    rotated_z = point_xyz[2] + scan_jitter[0, 2]
    inputs = jnp.concatenate([jnp.stack([rotated_x, rotated_y, rotated_z]), point_attrs], axis=0)
    pre_act = point_layer(inputs, point_weight, point_bias)
    local_feat = jax.nn.silu(pre_act).astype(jnp.bfloat16).reshape(owners, SLOT_CAP, width_one)
    incoming, vox_rows = (
        lax.all_to_all(local_feat, "blk", split_axis=0, concat_axis=0, tiled=True),
        lax.all_to_all(vox_sent, "blk", split_axis=0, concat_axis=0, tiled=True),
    )
    features = incoming.reshape(-1, width_one)
    vox_flat = vox_rows.reshape(-1)
    counts = jax.ops.segment_sum(jnp.ones_like(vox_flat), vox_flat, voxels + 1)[:voxels]
    divisor = jnp.maximum(counts, 1).astype(jnp.float32)
    totals = jax.ops.segment_sum(features.astype(jnp.float32), vox_flat, voxels + 1)[:voxels]
    pooled = lax.optimization_barrier((totals / divisor[:, None]).astype(jnp.bfloat16))
    occupied = (counts > 0).astype(jnp.float32)[:, None]
    pooled_pad = with_faces(pooled.reshape(edge_len, edge_len, -1), width_one)
    act_one = conv_apply(pooled_pad, conv_one, width_one)
    hidden = (occupied * jax.nn.silu(act_one)).astype(jnp.bfloat16)
    hidden_pad = with_faces(hidden.reshape(edge_len, edge_len, -1), width_one)
    out_two = conv_apply(hidden_pad, conv_two, width_one)
    block_out = (occupied * out_two).astype(jnp.bfloat16).reshape(edge_len, edge_len, -1)
    grad_two = jnp.where(
        occupied > 0, out_grad.reshape(voxels, width_two), jnp.zeros((), jnp.bfloat16)
    )
    grad_two_pad = with_faces(grad_two.reshape(edge_len, edge_len, -1), width_two)
    grad_hidden = conv_apply(grad_two_pad, flipped(conv_two, width_one), width_two)
    part_two = kernel_grad(hidden_pad, grad_two, edge_len)
    grad_act = (occupied * grad_hidden * silu_slope(act_one)).astype(jnp.bfloat16)
    grad_act_pad = with_faces(grad_act.reshape(edge_len, edge_len, -1), width_one)
    grad_pooled = conv_apply(grad_act_pad, flipped(conv_one, width_one), width_one)
    part_one = kernel_grad(pooled_pad, grad_act, edge_len)
    one_total, two_total = lax.psum((part_one, part_two), ("blk", "rep"))
    grad_ext = jnp.concatenate([grad_pooled, jnp.zeros((1, width_one), jnp.float32)], axis=0)
    count_ext = jnp.concatenate([divisor, jnp.ones((1,), jnp.float32)])
    grad_feat = grad_ext[vox_flat] / count_ext[vox_flat][:, None]
    returned = lax.all_to_all(
        grad_feat.reshape(owners, SLOT_CAP, width_one),
        "blk",
        split_axis=0,
        concat_axis=0,
        tiled=True,
    )
    grad_pre = returned.reshape(-1, width_one) * silu_slope(pre_act)
    grad_inputs = back_layer(grad_pre, point_weight)
    attr_grad = grad_inputs[3:]
    jitter_grad = jnp.sum(grad_inputs[:3], axis=1)[None, :]
    return (block_out, attr_grad, jitter_grad, one_total, two_total)


def solution(mesh):
    in_specs = (
        P(None, ("blk", "rep")),
        P(None, ("blk", "rep")),
        P(("blk", "rep")),
        P(("blk", "rep"), None),
        P(("blk", "rep"), None),
        P(("blk", "rep")),
        P(),
        P(),
        P(),
        P(),
        P("rep", "blk", None),
    )
    out_specs = (P("rep", "blk", None), P(None, ("blk", "rep")), P(("blk", "rep"), None), P(), P())
    return jax.shard_map(shards, mesh=mesh, in_specs=in_specs, out_specs=out_specs, check_vma=False)
```

profile of v0, /device:TPU:0, one launch (start us, length us, event | category | flops | bytes accessed | tf_op | source)
XLA Modules:
  0.0 269.6 jit_solution(3016571241570396834)
XLA Ops:
  7.2 0.9 reshape.249
  8.0 1.3 compare_select_fusion
  9.4 7.3 %all-to-all-start = ((s32[8,1,64]{2,1,0:T(1,128)}), s32[8,1,64]{2,1,0:T(1,128)S(1)}, u32[]{:S(2)}, u32[]{:S(2)}) async-start(s32[8,1,64]{2,1,0:T(1,128)} %compare_select_fusion), calls=%async_computation | async-start | bytes 8192 | tf_op jit(solution)/shard_map/all_to_all | solution.py:117
  17.5 1.4 fusion.41
  18.8 2.8 %subtract_add_fusion = (f32[1,512]{1,0:T(1,128)S(1)}, f32[1,512]{1,0:T(1,128)S(1)}, f32[1,512]{1,0:T(1,128)S(1)}) fusion(f32[3,512]{1,0:T(4,128)} %param.11, f32[]{:T(128)} %bitcast.4, f32[]{:T(128)} %bitcast.3, f32[]{:T(128)} %bitcast.2, f32[]{:T(128)} %bitcast.5, f32[]{:T(128)} %bitcast.6), kind=kLoop, calls=%fused_computation.81 | loop fusion | flops 4608 | bytes 12308 | tf_op jit(solution)/shard_map/add | solution.py:109
  21.6 1.8 multiply_convert_fusion.3
  23.4 0.8 copy.39
  24.2 0.3 copy.40
  24.5 6.0 %all-to-all-start.1 = ((bf16[8,64,96]{2,1,0:T(8,128)(2,1)}), bf16[8,64,96]{2,1,0:T(8,128)(2,1)S(1)}, u32[]{:S(2)}, u32[]{:S(2)}) async-start(bf16[8,64,96]{2,1,0:T(8,128)(2,1)} %bitcast.7), calls=%async_computation.1 | async-start | bytes 262144 | tf_op jit(solution)/shard_map/all_to_all | solution.py:116
  30.6 0.5 broadcast.171
  31.1 0.7 reduce.15
  31.9 4.1 %scatter_custom_fusion = s32[513]{0:T(1024)S(1)} fusion(s32[512]{0:T(512)S(1)} %reshape.282, s32[512]{0:T(512)S(1)} %broadcast.146, s32[]{:T(128)} %constant.8.clone.1), kind=kCustom, calls=%fused_computation.82 | custom fusion | flops 512 | bytes 2056 | tf_op jit(solution)/shard_map/scatter-add | solution.py:121
  36.3 0.1 bitcast_select_fusion
  36.5 3.9 %collective-permute-start.8 = (bf16[8,1,1024]{2,1,0:T(2,128)(2,1)S(1)}, bf16[8,1,1024]{2,1,0:T(2,128)(2,1)S(1)}, u32[]{:S(2)}, u32[]{:S(2)}) collective-permute-start(bf16[8,1,1024]{2,1,0:T(2,128)(2,1)S(1)} %get-tuple-element.21), channel_id=1, source_target_pairs={{0,4},{4,8},{8,12},{12,16},{16,20},{20,24},{24,28},{1,5},{5,9},{9,... | collective-permute-start | bytes 49160 | tf_op jit(solution)/shard_map/ppermute | solution.py:17
  40.3 1.3 collective-permute-start.9
  41.7 0.3 collective-permute-done.8
  41.9 4.2 %collective-permute-done.9 = bf16[8,1,1024]{2,1,0:T(2,128)(2,1)S(1)} collective-permute-done((bf16[8,1,1024]{2,1,0:T(2,128)(2,1)S(1)}, bf16[8,1,1024]{2,1,0:T(2,128)(2,1)S(1)}, u32[]{:S(2)}, u32[]{:S(2)}) %collective-permute-start.9) | collective-permute-done | bytes 16416 | tf_op jit(solution)/shard_map/ppermute | solution.py:19
  46.2 1.3 collective-permute-start.10
  47.5 1.3 collective-permute-start.11
  48.8 0.7 copy.38
  49.5 2.3 gather_fusion.1
  51.8 0.7 div.43
  53.0 3.2 %scatter_custom_fusion.1 = f32[513,96]{1,0:T(8,128)S(1)} fusion(s32[512]{0:T(512)S(1)} %reshape.282, bf16[512,96]{1,0:T(8,128)(2,1)S(1)} %bitcast.68, f32[]{:T(128)} %constant.11.clone.1), kind=kCustom, calls=%fused_computation.28 | custom fusion | flops 98304 | bytes 328068 | tf_op jit(solution)/shard_map/scatter-add | solution.py:123
  56.2 0.1 fusion.11
  56.6 3.8 %collective-permute-start = (bf16[8,1,768]{2,1,0:T(2,128)(2,1)S(1)}, bf16[8,1,768]{2,1,0:T(2,128)(2,1)S(1)}, u32[]{:S(2)}, u32[]{:S(2)}) collective-permute-start(bf16[8,1,768]{2,1,0:T(2,128)(2,1)S(1)} %get-tuple-element.27), channel_id=1, source_target_pairs={{0,4},{4,8},{8,12},{12,16},{16,20},{20,24},{24,28},{1,5},{5,9},{9,... | collective-permute-start | bytes 36872 | tf_op jit(solution)/shard_map/ppermute | solution.py:17
  60.4 1.3 collective-permute-start.1
  61.9 4.2 %collective-permute-done.1 = bf16[8,1,768]{2,1,0:T(2,128)(2,1)S(1)} collective-permute-done((bf16[8,1,768]{2,1,0:T(2,128)(2,1)S(1)}, bf16[8,1,768]{2,1,0:T(2,128)(2,1)S(1)}, u32[]{:S(2)}, u32[]{:S(2)}) %collective-permute-start.1) | collective-permute-done | bytes 12320 | tf_op jit(solution)/shard_map/ppermute | solution.py:19
  66.2 3.8 %collective-permute-start.2 = (bf16[1,10,768]{2,1,0:T(8,128)(2,1)S(1)}, bf16[1,10,768]{2,1,0:T(8,128)(2,1)S(1)}, u32[]{:S(2)}, u32[]{:S(2)}) collective-permute-start(bf16[1,10,768]{2,1,0:T(8,128)(2,1)S(1)} %get-tuple-element.19), channel_id=1, source_target_pairs={{0,1},{1,2},{2,3},{4,5},{5,6},{6,7},{8,9},{9,10},{10,11},{12,13},{... | collective-permute-start | bytes 46088 | tf_op jit(solution)/shard_map/ppermute | solution.py:17
  70.0 1.5 collective-permute-start.3
  71.5 0.5 broadcast.172
  72.0 4.0 %fusion.43 = (f32[8,8,8,96]{3,2,1,0:T(8,128)S(1)}, f32[1,8,8,8,96]{4,0,3,2,1:T(1,128)S(1)}) fusion(f32[]{:T(128)} %broadcast.172, bf16[3,3,3,96,128]{4,3,2,1,0:T(8,128)(2,1)S(1)} %bitcast.61, bf16[1,10,10,10,128]{4,3,2,1,0:T(8,128)(2,1)S(1)} %pad_bitcast_fusion.5), kind=kOutput, calls=%fused_computation.94 | convolution fusion | flops 339738624 | bytes 1312772 | tf_op jit(solution)/shard_map/conv_general_dilated | solution.py:54
  76.2 0.3 reshape.252
  76.5 0.1 pad_bitcast_fusion.2
  76.7 4.2 %fusion.42 = (f32[8,8,8,96]{3,2,1,0:T(8,128)S(1)}, f32[1,8,8,8,96]{4,0,3,2,1:T(1,128)S(1)}) fusion(f32[]{:T(128)} %broadcast.172, bf16[3,3,3,96,96]{4,3,2,1,0:T(8,128)(2,1)S(1)} %bitcast.66, bf16[1,10,10,10,96]{4,3,2,1,0:T(8,128)(2,1)S(1)} %get-tuple-element.12), kind=kOutput, calls=%fused_computation.93 | convolution fusion | flops 254803968 | bytes 1082884 | tf_op jit(solution)/shard_map/conv_general_dilated | solution.py:54
  81.1 3.2 %collective-permute-start.12 = (bf16[8,1,768]{2,1,0:T(2,128)(2,1)S(1)}, bf16[8,1,768]{2,1,0:T(2,128)(2,1)S(1)}, u32[]{:S(2)}, u32[]{:S(2)}) collective-permute-start(bf16[8,1,768]{2,1,0:T(2,128)(2,1)S(1)} %get-tuple-element.23), channel_id=1, source_target_pairs={{0,4},{4,8},{8,12},{12,16},{16,20},{20,24},{24,28},{1,5},{5,9},{9,... | collective-permute-start | bytes 36872 | tf_op jit(solution)/shard_map/ppermute | solution.py:17
  84.3 1.3 collective-permute-start.13
  85.6 4.5 %collective-permute-start.4 = (bf16[8,1,768]{2,1,0:T(2,128)(2,1)S(1)}, bf16[8,1,768]{2,1,0:T(2,128)(2,1)S(1)}, u32[]{:S(2)}, u32[]{:S(2)}) collective-permute-start(bf16[8,1,768]{2,1,0:T(2,128)(2,1)S(1)} %get-tuple-element.25), channel_id=1, source_target_pairs={{0,4},{4,8},{8,12},{12,16},{16,20},{20,24},{24,28},{1,5},{5,9},{9,... | collective-permute-start | bytes 36872 | tf_op jit(solution)/shard_map/ppermute | solution.py:17
  90.2 1.3 collective-permute-start.5
  91.5 0.1 multiply_convert_fusion
  91.7 3.6 %fusion.2 = f32[3,3,3,96,96]{4,3,2,1,0:T(8,128)S(1)} fusion(bf16[96,10,10,10,1]{0,3,4,2,1:T(8,128)(2,1)S(1)} %get-tuple-element.11, bf16[8,8,8,1,96]{4,2,1,0,3:T(8,128)(2,1)S(1)} %multiply_convert_fusion), kind=kOutput, calls=%fused_computation.10 | convolution fusion | flops 254803968 | bytes 1285632 | tf_op jit(solution)/shard_map/transpose | solution.py:78
  95.2 1.4 copy.49
  96.6 5.1 %collective-permute-start.14 = (bf16[1,10,768]{2,1,0:T(8,128)(2,1)S(1)}, bf16[1,10,768]{2,1,0:T(8,128)(2,1)S(1)}, u32[]{:S(2)}, u32[]{:S(2)}) collective-permute-start(bf16[1,10,768]{2,1,0:T(8,128)(2,1)S(1)} %get-tuple-element.15), channel_id=1, source_target_pairs={{0,1},{1,2},{2,3},{4,5},{5,6},{6,7},{8,9},{9,10},{10,11},{12,13},{... | collective-permute-start | bytes 46088 | tf_op jit(solution)/shard_map/ppermute | solution.py:17
  101.8 1.3 collective-permute-start.15
  103.1 5.1 %collective-permute-start.6 = (bf16[1,10,768]{2,1,0:T(8,128)(2,1)S(1)}, bf16[1,10,768]{2,1,0:T(8,128)(2,1)S(1)}, u32[]{:S(2)}, u32[]{:S(2)}) collective-permute-start(bf16[1,10,768]{2,1,0:T(8,128)(2,1)S(1)} %get-tuple-element.17), channel_id=1, source_target_pairs={{0,1},{1,2},{2,3},{4,5},{5,6},{6,7},{8,9},{9,10},{10,11},{12,13},{... | collective-permute-start | bytes 46088 | tf_op jit(solution)/shard_map/ppermute | solution.py:17
  108.2 1.5 collective-permute-start.7
  109.9 0.3 reshape.257
  110.2 2.4 collective-permute-done.7
  112.7 0.3 reshape.254
  113.1 0.1 pad_bitcast_fusion
  113.2 4.9 %fusion = f32[3,3,3,96,128]{4,3,2,1,0:T(8,128)} fusion(bf16[96,10,10,10,1]{0,3,4,2,1:T(8,128)(2,1)S(1)} %get-tuple-element.9, pred[8,8,8]{2,1,0:T(8,128)(4,1)S(1)} %broadcast_compare_fusion, bf16[8,8,8,1,128]{4,1,2,0,3:T(8,128)(2,1)S(1)} %bitcast.72), kind=kOutput, calls=%fused_computation.8 | convolution fusion | flops 339804160 | bytes 1650688 | tf_op jit(solution)/shard_map/transpose | solution.py:78
  118.1 1.1 copy-done.3
  119.2 5.5 %fusion.4 = f32[1,8,8,8,96]{4,0,3,2,1:T(1,128)S(1)} fusion(bf16[3,3,3,96,96]{4,3,2,1,0:T(8,128)(2,1)S(1)} %bitcast.67, bf16[1,10,10,10,96]{4,3,2,1,0:T(8,128)(2,1)S(1)} %pad_bitcast_fusion.4), kind=kOutput, calls=%fused_computation.12 | convolution fusion | flops 254803968 | bytes 886272 | tf_op jit(solution)/shard_map/conv_general_dilated | solution.py:54
  124.7 1.0 gather_fusion
  125.8 0.9 broadcast_divide_fusion
  126.6 6.4 %all-to-all-start.2 = ((f32[8,64,96]{2,1,0:T(8,128)}), f32[8,64,96]{2,1,0:T(8,128)S(1)}, u32[]{:S(2)}, u32[]{:S(2)}) async-start(f32[8,64,96]{2,1,0:T(8,128)} %broadcast_divide_fusion), calls=%async_computation.2 | async-start | bytes 524288 | tf_op jit(solution)/shard_map/all_to_all | solution.py:146
  133.1 3.4 %convolution_reduce_fusion = f32[8,8,8,128]{3,2,1,0:T(8,128)S(1)} fusion(bf16[3,3,3,96,128]{4,3,2,1,0:T(8,128)(2,1)S(1)} %bitcast.60, bf16[1,10,10,10,96]{4,3,2,1,0:T(8,128)(2,1)S(1)} %get-tuple-element.10), kind=kOutput, calls=%fused_computation.4 | convolution fusion | flops 339738624 | bytes 1117696 | tf_op jit(solution)/shard_map/conv_general_dilated | solution.py:54
  136.6 0.8 fusion.14
  137.3 6.9 %all-to-all-done.2 = f32[8,64,96]{2,1,0:T(8,128)S(1)} async-done(((f32[8,64,96]{2,1,0:T(8,128)}), f32[8,64,96]{2,1,0:T(8,128)S(1)}, u32[]{:S(2)}, u32[]{:S(2)}) %all-to-all-start.2) | async-done | bytes 196640 | tf_op jit(solution)/shard_map/all_to_all | solution.py:146
  144.4 0.3 convolution_bitcast_fusion
  144.7 0.6 slice.119
  145.3 0.6 slice_reduce_fusion
  146.0 113.4 %all-reduce.8.cloned.1.call-done = (f32[2592,96]{0,1:T(8,128)}, f32[2592,128]{1,0:T(8,128)}) async-done(((f32[2592,96]{0,1:T(8,128)}, f32[2592,128]{1,0:T(8,128)}), (f32[2592,96]{0,1:T(8,128)}, f32[2592,128]{1,0:T(8,128)})) %all-reduce.8.cloned.1.call-update) | async-done | bytes 2322448 | tf_op jit(solution)/shard_map/psum | solution.py:142
  259.4 2.3 copy.77
  261.7 1.1 copy.78
  (74 shorter events, 2.6 us)
Async XLA Ops:
  7.2 64.3 %copy-start = (bf16[2592,128]{1,0:T(8,128)(2,1)S(1)}, bf16[2592,128]{1,0:T(8,128)(2,1)}, u32[]{:S(2)}) copy-start(bf16[2592,128]{1,0:T(8,128)(2,1)} %param.20) | copy-start | bytes 1990660
  7.2 17.0 %copy-start.4 = (bf16[2592,96]{0,1:T(8,128)(2,1)S(1)}, bf16[2592,96]{0,1:T(8,128)(2,1)}, u32[]{:S(2)}) copy-start(bf16[2592,96]{0,1:T(8,128)(2,1)} %param.19) | copy-start | bytes 1492996
  9.4 15.2 %all-to-all-start = ((s32[8,1,64]{2,1,0:T(1,128)}), s32[8,1,64]{2,1,0:T(1,128)S(1)}, u32[]{:S(2)}, u32[]{:S(2)}) async-start(s32[8,1,64]{2,1,0:T(1,128)} %compare_select_fusion), calls=%async_computation | async-start | bytes 8192 | tf_op jit(solution)/shard_map/all_to_all | solution.py:117
  21.6 14.7 %copy-start.5 = (bf16[8,8,1024]{2,1,0:T(8,128)(2,1)S(1)}, bf16[8,8,1024]{2,1,0:T(8,128)(2,1)}, u32[]{:S(2)}) copy-start(bf16[8,8,1024]{2,1,0:T(8,128)(2,1)} %param.21) | copy-start | bytes 393220
  24.5 52.1 %copy-start.2 = (bf16[2592,96]{1,0:T(8,128)(2,1)}, bf16[2592,96]{1,0:T(8,128)(2,1)S(1)}, u32[]{:S(2)}) copy-start(bf16[2592,96]{1,0:T(8,128)(2,1)S(1)} %copy.40) | copy-start | bytes 1492996
  24.5 28.5 %all-to-all-start.1 = ((bf16[8,64,96]{2,1,0:T(8,128)(2,1)}), bf16[8,64,96]{2,1,0:T(8,128)(2,1)S(1)}, u32[]{:S(2)}, u32[]{:S(2)}) async-start(bf16[8,64,96]{2,1,0:T(8,128)(2,1)} %bitcast.7), calls=%async_computation.1 | async-start | bytes 262144 | tf_op jit(solution)/shard_map/all_to_all | solution.py:116
  30.5 228.8 %all-reduce.8.cloned.1.call-start = ((), (), s32[]{:S(2)}) async-start(), calls=%async_computation.3 | async-start | bytes 4718592 | tf_op jit(solution)/shard_map/psum | solution.py:142
  36.5 5.5 %collective-permute-start.8 = (bf16[8,1,1024]{2,1,0:T(2,128)(2,1)S(1)}, bf16[8,1,1024]{2,1,0:T(2,128)(2,1)S(1)}, u32[]{:S(2)}, u32[]{:S(2)}) collective-permute-start(bf16[8,1,1024]{2,1,0:T(2,128)(2,1)S(1)} %get-tuple-element.21), channel_id=1, source_target_pairs={{0,4},{4,8},{8,12},{12,16},{16,20},{20,24},{24,28},{1,5},{5,9},{9,... | collective-permute-start | bytes 49160 | tf_op jit(solution)/shard_map/ppermute | solution.py:17
  40.3 5.8 %collective-permute-start.9 = (bf16[8,1,1024]{2,1,0:T(2,128)(2,1)S(1)}, bf16[8,1,1024]{2,1,0:T(2,128)(2,1)S(1)}, u32[]{:S(2)}, u32[]{:S(2)}) collective-permute-start(bf16[8,1,1024]{2,1,0:T(2,128)(2,1)S(1)} %get-tuple-element.22), channel_id=1, source_target_pairs={{4,0},{8,4},{12,8},{16,12},{20,16},{24,20},{28,24},{5,1},{9,5},{13... | collective-permute-start | bytes 49160 | tf_op jit(solution)/shard_map/ppermute | solution.py:19
  41.7 10.8 %copy-start.8 = (s32[1024]{0:T(1024)}, s32[1024]{0:T(1024)S(1)}, u32[]{:S(2)}) copy-start(s32[1024]{0:T(1024)S(1)} %pad_clamp_fusion) | copy-start | bytes 12292
  46.2 6.5 %collective-permute-start.10 = (bf16[1,10,1024]{2,1,0:T(8,128)(2,1)S(1)}, bf16[1,10,1024]{2,1,0:T(8,128)(2,1)S(1)}, u32[]{:S(2)}, u32[]{:S(2)}) collective-permute-start(bf16[1,10,1024]{2,1,0:T(8,128)(2,1)S(1)} %get-tuple-element.13), channel_id=1, source_target_pairs={{0,1},{1,2},{2,3},{4,5},{5,6},{6,7},{8,9},{9,10},{10,11},{12,13},{... | collective-permute-start | bytes 61448 | tf_op jit(solution)/shard_map/ppermute | solution.py:17
  47.5 5.2 %collective-permute-start.11 = (bf16[1,10,1024]{2,1,0:T(8,128)(2,1)S(1)}, bf16[1,10,1024]{2,1,0:T(8,128)(2,1)S(1)}, u32[]{:S(2)}, u32[]{:S(2)}) collective-permute-start(bf16[1,10,1024]{2,1,0:T(8,128)(2,1)S(1)} %get-tuple-element.14), channel_id=1, source_target_pairs={{1,0},{2,1},{3,2},{5,4},{6,5},{7,6},{9,8},{10,9},{11,10},{13,12},{... | collective-permute-start | bytes 61448 | tf_op jit(solution)/shard_map/ppermute | solution.py:19
  56.6 5.3 %collective-permute-start = (bf16[8,1,768]{2,1,0:T(2,128)(2,1)S(1)}, bf16[8,1,768]{2,1,0:T(2,128)(2,1)S(1)}, u32[]{:S(2)}, u32[]{:S(2)}) collective-permute-start(bf16[8,1,768]{2,1,0:T(2,128)(2,1)S(1)} %get-tuple-element.27), channel_id=1, source_target_pairs={{0,4},{4,8},{8,12},{12,16},{16,20},{20,24},{24,28},{1,5},{5,9},{9,... | collective-permute-start | bytes 36872 | tf_op jit(solution)/shard_map/ppermute | solution.py:17
  60.4 5.7 %collective-permute-start.1 = (bf16[8,1,768]{2,1,0:T(2,128)(2,1)S(1)}, bf16[8,1,768]{2,1,0:T(2,128)(2,1)S(1)}, u32[]{:S(2)}, u32[]{:S(2)}) collective-permute-start(bf16[8,1,768]{2,1,0:T(2,128)(2,1)S(1)} %get-tuple-element.28), channel_id=1, source_target_pairs={{4,0},{8,4},{12,8},{16,12},{20,16},{24,20},{28,24},{5,1},{9,5},{13... | collective-permute-start | bytes 36872 | tf_op jit(solution)/shard_map/ppermute | solution.py:19
  66.2 10.0 %collective-permute-start.2 = (bf16[1,10,768]{2,1,0:T(8,128)(2,1)S(1)}, bf16[1,10,768]{2,1,0:T(8,128)(2,1)S(1)}, u32[]{:S(2)}, u32[]{:S(2)}) collective-permute-start(bf16[1,10,768]{2,1,0:T(8,128)(2,1)S(1)} %get-tuple-element.19), channel_id=1, source_target_pairs={{0,1},{1,2},{2,3},{4,5},{5,6},{6,7},{8,9},{9,10},{10,11},{12,13},{... | collective-permute-start | bytes 46088 | tf_op jit(solution)/shard_map/ppermute | solution.py:17
  70.0 6.2 %collective-permute-start.3 = (bf16[1,10,768]{2,1,0:T(8,128)(2,1)S(1)}, bf16[1,10,768]{2,1,0:T(8,128)(2,1)S(1)}, u32[]{:S(2)}, u32[]{:S(2)}) collective-permute-start(bf16[1,10,768]{2,1,0:T(8,128)(2,1)S(1)} %get-tuple-element.20), channel_id=1, source_target_pairs={{1,0},{2,1},{3,2},{5,4},{6,5},{7,6},{9,8},{10,9},{11,10},{13,12},{... | collective-permute-start | bytes 46088 | tf_op jit(solution)/shard_map/ppermute | solution.py:19
  81.1 15.5 %collective-permute-start.12 = (bf16[8,1,768]{2,1,0:T(2,128)(2,1)S(1)}, bf16[8,1,768]{2,1,0:T(2,128)(2,1)S(1)}, u32[]{:S(2)}, u32[]{:S(2)}) collective-permute-start(bf16[8,1,768]{2,1,0:T(2,128)(2,1)S(1)} %get-tuple-element.23), channel_id=1, source_target_pairs={{0,4},{4,8},{8,12},{12,16},{16,20},{20,24},{24,28},{1,5},{5,9},{9,... | collective-permute-start | bytes 36872 | tf_op jit(solution)/shard_map/ppermute | solution.py:17
  84.3 12.3 %collective-permute-start.13 = (bf16[8,1,768]{2,1,0:T(2,128)(2,1)S(1)}, bf16[8,1,768]{2,1,0:T(2,128)(2,1)S(1)}, u32[]{:S(2)}, u32[]{:S(2)}) collective-permute-start(bf16[8,1,768]{2,1,0:T(2,128)(2,1)S(1)} %get-tuple-element.24), channel_id=1, source_target_pairs={{4,0},{8,4},{12,8},{16,12},{20,16},{24,20},{28,24},{5,1},{9,5},{13... | collective-permute-start | bytes 36872 | tf_op jit(solution)/shard_map/ppermute | solution.py:19
  85.6 17.4 %collective-permute-start.4 = (bf16[8,1,768]{2,1,0:T(2,128)(2,1)S(1)}, bf16[8,1,768]{2,1,0:T(2,128)(2,1)S(1)}, u32[]{:S(2)}, u32[]{:S(2)}) collective-permute-start(bf16[8,1,768]{2,1,0:T(2,128)(2,1)S(1)} %get-tuple-element.25), channel_id=1, source_target_pairs={{0,4},{4,8},{8,12},{12,16},{16,20},{20,24},{24,28},{1,5},{5,9},{9,... | collective-permute-start | bytes 36872 | tf_op jit(solution)/shard_map/ppermute | solution.py:17
  90.2 12.9 %collective-permute-start.5 = (bf16[8,1,768]{2,1,0:T(2,128)(2,1)S(1)}, bf16[8,1,768]{2,1,0:T(2,128)(2,1)S(1)}, u32[]{:S(2)}, u32[]{:S(2)}) collective-permute-start(bf16[8,1,768]{2,1,0:T(2,128)(2,1)S(1)} %get-tuple-element.26), channel_id=1, source_target_pairs={{4,0},{8,4},{12,8},{16,12},{20,16},{24,20},{28,24},{5,1},{9,5},{13... | collective-permute-start | bytes 36872 | tf_op jit(solution)/shard_map/ppermute | solution.py:19
  96.6 13.1 %collective-permute-start.14 = (bf16[1,10,768]{2,1,0:T(8,128)(2,1)S(1)}, bf16[1,10,768]{2,1,0:T(8,128)(2,1)S(1)}, u32[]{:S(2)}, u32[]{:S(2)}) collective-permute-start(bf16[1,10,768]{2,1,0:T(8,128)(2,1)S(1)} %get-tuple-element.15), channel_id=1, source_target_pairs={{0,1},{1,2},{2,3},{4,5},{5,6},{6,7},{8,9},{9,10},{10,11},{12,13},{... | collective-permute-start | bytes 46088 | tf_op jit(solution)/shard_map/ppermute | solution.py:17
  101.8 8.0 %collective-permute-start.15 = (bf16[1,10,768]{2,1,0:T(8,128)(2,1)S(1)}, bf16[1,10,768]{2,1,0:T(8,128)(2,1)S(1)}, u32[]{:S(2)}, u32[]{:S(2)}) collective-permute-start(bf16[1,10,768]{2,1,0:T(8,128)(2,1)S(1)} %get-tuple-element.16), channel_id=1, source_target_pairs={{1,0},{2,1},{3,2},{5,4},{6,5},{7,6},{9,8},{10,9},{11,10},{13,12},{... | collective-permute-start | bytes 46088 | tf_op jit(solution)/shard_map/ppermute | solution.py:19
  103.1 7.0 %collective-permute-start.6 = (bf16[1,10,768]{2,1,0:T(8,128)(2,1)S(1)}, bf16[1,10,768]{2,1,0:T(8,128)(2,1)S(1)}, u32[]{:S(2)}, u32[]{:S(2)}) collective-permute-start(bf16[1,10,768]{2,1,0:T(8,128)(2,1)S(1)} %get-tuple-element.17), channel_id=1, source_target_pairs={{0,1},{1,2},{2,3},{4,5},{5,6},{6,7},{8,9},{9,10},{10,11},{12,13},{... | collective-permute-start | bytes 46088 | tf_op jit(solution)/shard_map/ppermute | solution.py:17
  108.2 4.3 %collective-permute-start.7 = (bf16[1,10,768]{2,1,0:T(8,128)(2,1)S(1)}, bf16[1,10,768]{2,1,0:T(8,128)(2,1)S(1)}, u32[]{:S(2)}, u32[]{:S(2)}) collective-permute-start(bf16[1,10,768]{2,1,0:T(8,128)(2,1)S(1)} %get-tuple-element.18), channel_id=1, source_target_pairs={{1,0},{2,1},{3,2},{5,4},{6,5},{7,6},{9,8},{10,9},{11,10},{13,12},{... | collective-permute-start | bytes 46088 | tf_op jit(solution)/shard_map/ppermute | solution.py:19
  118.1 1.1 copy-start.3
  119.2 5.5 %copy-start.9 = (s32[1024]{0:T(1024)S(1)}, s32[1024]{0:T(1024)}, u32[]{:S(2)}) copy-start(s32[1024]{0:T(1024)} %copy-done.8) | copy-start | bytes 12292
  124.7 1.1 copy-start.7
  126.6 17.7 %all-to-all-start.2 = ((f32[8,64,96]{2,1,0:T(8,128)}), f32[8,64,96]{2,1,0:T(8,128)S(1)}, u32[]{:S(2)}, u32[]{:S(2)}) async-start(f32[8,64,96]{2,1,0:T(8,128)} %broadcast_divide_fusion), calls=%async_computation.2 | async-start | bytes 524288 | tf_op jit(solution)/shard_map/all_to_all | solution.py:146
  133.1 3.5 %copy-start.6 = (f32[8,8,8]{1,2,0:T(8,128)S(1)}, f32[8,8,8]{1,2,0:T(8,128)}, u32[]{:S(2)}) copy-start(f32[8,8,8]{1,2,0:T(8,128)} %copy.38) | copy-start | bytes 6148
  136.5 7.9 %copy-start.10 = (f32[8,96]{1,0:T(8,128)S(1)}, f32[8,96]{1,0:T(8,128)}, u32[]{:S(2)}) copy-start(f32[8,96]{1,0:T(8,128)} %param.17) | copy-start | bytes 9220
  136.5 7.9 %copy-start.11 = (f32[512,96]{0,1:T(8,128)S(1)}, f32[512,96]{0,1:T(8,128)}, u32[]{:S(2)}) copy-start(f32[512,96]{0,1:T(8,128)} %get-tuple-element.36) | copy-start | bytes 589828
  259.4 2.4 copy-start.1
Sparse Core Ops, SparseCore 0:
  118.2 141.0 all-reduce.7
where the time goes:
time: 271 us; the launch traced here: 270 us
  waiting for transfers between devices  132 us (49%)
  starting transfers between devices  61.3 us (23%)
  matrix products  27.6 us (10%)
  local copies, waits for them, and re-layouts  18.2 us (7%)
  between operations  15.5 us (6%)
  other arithmetic  15.4 us (6%)
    psum x1, waiting for transfers between devices, shards(): one_total, two_total = lax.psum((part_one, part_two), ('blk', 'rep'))  113 us
    ppermute x8, starting transfers between devices, with_halo(): lax.ppermute(tail, axis, [(i, (i + 1) % count) for i in range(ends)])  30.7 us
    conv_general_dilated x4, matrix products, conv_apply(): lax.conv_general_dilated(padded[None], kernel, (1, 1, 1), 'VALID', dimens...  17 us
    ppermute x8, waiting for transfers between devices, with_halo(): lax.ppermute(head, axis, [((i + 1) % count, i) for i in range(ends)])  10.9 us
    ppermute x8, starting transfers between devices, with_halo(): lax.ppermute(head, axis, [((i + 1) % count, i) for i in range(ends)])  10.7 us
    transpose x2, matrix products, kernel_grad(): jnp.transpose(result, (1, 2, 3, 0, 4))  8.46 us
    all_to_all x1, starting transfers between devices, shards(): lax.all_to_all(vox_sent, 'blk', split_axis=0, concat_axis=0, tiled=True)  7.31 us
    all_to_all x1, waiting for transfers between devices, shards(): lax.all_to_all(grad_feat.reshape(owners, SLOT_CAP, width_one), 'blk', spl...  6.94 us
  transfers between devices with their start and end apart: 20, of which 7 were waited for; matrix products, arithmetic and copies ran while one was open for 15% of the time, Pallas kernels for 0%

commit v1 on v0

--- a/solution.py
+++ b/solution.py
@@ -139,7 +139,9 @@
     grad_act_pad = with_faces(grad_act.reshape(edge_len, edge_len, -1), width_one)
     grad_pooled = conv_apply(grad_act_pad, flipped(conv_one, width_one), width_one)
     part_one = kernel_grad(pooled_pad, grad_act, edge_len)
-    one_total, two_total = lax.psum((part_one, part_two), ("blk", "rep"))
+    one_total, two_total = jax.lax.psum(
+        jax.lax.psum((part_one, part_two), axis_name="rep"), axis_name="blk"
+    )
     grad_ext = jnp.concatenate([grad_pooled, jnp.zeros((1, width_one), jnp.float32)], axis=0)
     count_ext = jnp.concatenate([divisor, jnp.ones((1,), jnp.float32)])
     grad_feat = grad_ext[vox_flat] / count_ext[vox_flat][:, None]

time: 271 us -> 291 us (1.074)
  waiting for transfers between devices: 132 us -> 161 us
  starting transfers between devices: 61.3 us -> 52.2 us
    psum x1 -> x2, waiting for transfers between devices: 113 us -> 134 us  [the longest x1 79.3 us: shards(): jax.lax.psum(jax.lax.psum((part_one, part_two), axis_name='rep'), axis_na...]
    ppermute x8, starting transfers between devices: 30.7 us -> 21.6 us  [with_halo(): lax.ppermute(tail, axis, [(i, (i + 1) % count) for i in range(ends)])]
    all_to_all x1, waiting for transfers between devices: 6.94 us -> 13.5 us  [shards(): lax.all_to_all(grad_feat.reshape(owners, SLOT_CAP, width_one), 'blk', spl...]
  transfers between devices with their start and end apart: 20 -> 21, of which waited for: 7 -> 9; matrix products, arithmetic and copies ran while one was open for 15% -> 12% of each run, Pallas kernels for 0% -> 0%
where the time goes in v1:
time: 291 us; the launch traced here: 290 us
  waiting for transfers between devices  161 us (55%)
  starting transfers between devices  52.2 us (18%)
  matrix products  27.5 us (9%)
  local copies, waits for them, and re-layouts  17.1 us (6%)
  other arithmetic  16.9 us (6%)
  between operations  15.5 us (5%)
    psum x1, waiting for transfers between devices, shards(): jax.lax.psum(jax.lax.psum((part_one, part_two), axis_name='rep'), axis_na...  79.3 us
    psum x1, waiting for transfers between devices, shards(): jax.lax.psum((part_one, part_two), axis_name='rep')  54.3 us
    ppermute x8, starting transfers between devices, with_halo(): lax.ppermute(tail, axis, [(i, (i + 1) % count) for i in range(ends)])  21.6 us
    conv_general_dilated x4, matrix products, conv_apply(): lax.conv_general_dilated(padded[None], kernel, (1, 1, 1), 'VALID', dimens...  17.1 us
    all_to_all x1, waiting for transfers between devices, shards(): lax.all_to_all(grad_feat.reshape(owners, SLOT_CAP, width_one), 'blk', spl...  13.5 us
    ppermute x8, waiting for transfers between devices, with_halo(): lax.ppermute(head, axis, [((i + 1) % count, i) for i in range(ends)])  11.9 us
    ppermute x8, starting transfers between devices, with_halo(): lax.ppermute(head, axis, [((i + 1) % count, i) for i in range(ends)])  11 us
    transpose x2, matrix products, kernel_grad(): jnp.transpose(result, (1, 2, 3, 0, 4))  8.36 us
  transfers between devices with their start and end apart: 21, of which 9 were waited for; matrix products, arithmetic and copies ran while one was open for 12% of the time, Pallas kernels for 0%

profile of v1, /device:TPU:0, one launch (start us, length us, event | category | flops | bytes accessed | tf_op | source)
XLA Modules:
  0.0 290.4 jit_solution(6332117913405881907)
XLA Ops:
  7.2 0.9 reshape.249
  8.0 1.3 compare_select_fusion
  9.4 7.3 %all-to-all-start = ((s32[8,1,64]{2,1,0:T(1,128)}), s32[8,1,64]{2,1,0:T(1,128)S(1)}, u32[]{:S(2)}, u32[]{:S(2)}) async-start(s32[8,1,64]{2,1,0:T(1,128)} %compare_select_fusion), calls=%async_computation | async-start | bytes 8192 | tf_op jit(solution)/shard_map/all_to_all | solution.py:117
  17.5 1.4 fusion.41
  18.8 2.8 subtract_add_fusion
  21.6 1.5 all-to-all-done
  23.1 0.5 broadcast.171
  23.6 0.7 reduce.15
  24.4 4.1 %scatter_custom_fusion = s32[513]{0:T(1024)S(1)} fusion(s32[512]{0:T(512)S(1)} %reshape.282, s32[512]{0:T(512)S(1)} %broadcast.146, s32[]{:T(128)} %constant.8.clone.1), kind=kCustom, calls=%fused_computation.82 | custom fusion | flops 512 | bytes 2056 | tf_op jit(solution)/shard_map/scatter-add | solution.py:121
  28.7 1.0 bitcast_select_fusion
  29.8 2.5 collective-permute-start.8
  32.2 1.3 collective-permute-start.9
  33.5 1.8 multiply_convert_fusion.3
  35.3 0.8 copy.39
  36.1 6.6 %all-to-all-start.1 = ((bf16[8,64,96]{2,1,0:T(8,128)(2,1)}), bf16[8,64,96]{2,1,0:T(8,128)(2,1)S(1)}, u32[]{:S(2)}, u32[]{:S(2)}) async-start(bf16[8,64,96]{2,1,0:T(8,128)(2,1)} %bitcast.7), calls=%async_computation.1 | async-start | bytes 262144 | tf_op jit(solution)/shard_map/all_to_all | solution.py:116
  42.8 0.3 copy.40
  43.2 1.3 collective-permute-start.10
  44.5 1.3 collective-permute-start.11
  46.1 3.2 %collective-permute-done.11 = bf16[1,10,1024]{2,1,0:T(8,128)(2,1)S(1)} collective-permute-done((bf16[1,10,1024]{2,1,0:T(8,128)(2,1)S(1)}, bf16[1,10,1024]{2,1,0:T(8,128)(2,1)S(1)}, u32[]{:S(2)}, u32[]{:S(2)}) %collective-permute-start.11) | collective-permute-done | bytes 20512 | tf_op jit(solution)/shard_map/ppermute | solution.py:19
  49.6 0.5 all-to-all-done.1
  50.1 3.2 %scatter_custom_fusion.1 = f32[513,96]{1,0:T(8,128)S(1)} fusion(s32[512]{0:T(512)S(1)} %reshape.282, bf16[512,96]{1,0:T(8,128)(2,1)S(1)} %bitcast.68, f32[]{:T(128)} %constant.11.clone.1), kind=kCustom, calls=%fused_computation.28 | custom fusion | flops 98304 | bytes 328068 | tf_op jit(solution)/shard_map/scatter-add | solution.py:123
  53.3 0.1 fusion.11
  53.6 3.0 %collective-permute-start = (bf16[8,1,768]{2,1,0:T(2,128)(2,1)S(1)}, bf16[8,1,768]{2,1,0:T(2,128)(2,1)S(1)}, u32[]{:S(2)}, u32[]{:S(2)}) collective-permute-start(bf16[8,1,768]{2,1,0:T(2,128)(2,1)S(1)} %get-tuple-element.29), channel_id=1, source_target_pairs={{0,4},{4,8},{8,12},{12,16},{16,20},{20,24},{24,28},{1,5},{5,9},{9,... | collective-permute-start | bytes 36872 | tf_op jit(solution)/shard_map/ppermute | solution.py:17
  56.6 1.3 collective-permute-start.1
  58.1 4.4 %collective-permute-done.1 = bf16[8,1,768]{2,1,0:T(2,128)(2,1)S(1)} collective-permute-done((bf16[8,1,768]{2,1,0:T(2,128)(2,1)S(1)}, bf16[8,1,768]{2,1,0:T(2,128)(2,1)S(1)}, u32[]{:S(2)}, u32[]{:S(2)}) %collective-permute-start.1) | collective-permute-done | bytes 12320 | tf_op jit(solution)/shard_map/ppermute | solution.py:19
  62.6 3.4 %collective-permute-start.2 = (bf16[1,10,768]{2,1,0:T(8,128)(2,1)S(1)}, bf16[1,10,768]{2,1,0:T(8,128)(2,1)S(1)}, u32[]{:S(2)}, u32[]{:S(2)}) collective-permute-start(bf16[1,10,768]{2,1,0:T(8,128)(2,1)S(1)} %get-tuple-element.21), channel_id=1, source_target_pairs={{0,1},{1,2},{2,3},{4,5},{5,6},{6,7},{8,9},{9,10},{10,11},{12,13},{... | collective-permute-start | bytes 46088 | tf_op jit(solution)/shard_map/ppermute | solution.py:17
  65.9 1.5 collective-permute-start.3
  67.4 0.5 broadcast.172
  67.9 4.0 %fusion.43 = (f32[8,8,8,96]{3,2,1,0:T(8,128)S(1)}, f32[1,8,8,8,96]{4,0,3,2,1:T(1,128)S(1)}) fusion(f32[]{:T(128)} %broadcast.172, bf16[3,3,3,96,128]{4,3,2,1,0:T(8,128)(2,1)S(1)} %bitcast.61, bf16[1,10,10,10,128]{4,3,2,1,0:T(8,128)(2,1)S(1)} %pad_bitcast_fusion.5), kind=kOutput, calls=%fused_computation.94 | convolution fusion | flops 339738624 | bytes 1312772 | tf_op jit(solution)/shard_map/conv_general_dilated | solution.py:54
  72.2 0.3 reshape.252
  72.6 4.1 %fusion.42 = (f32[8,8,8,96]{3,2,1,0:T(8,128)S(1)}, f32[1,8,8,8,96]{4,0,3,2,1:T(1,128)S(1)}) fusion(f32[]{:T(128)} %broadcast.172, bf16[3,3,3,96,96]{4,3,2,1,0:T(8,128)(2,1)S(1)} %bitcast.66, bf16[1,10,10,10,96]{4,3,2,1,0:T(8,128)(2,1)S(1)} %get-tuple-element.14), kind=kOutput, calls=%fused_computation.93 | convolution fusion | flops 254803968 | bytes 1082884 | tf_op jit(solution)/shard_map/conv_general_dilated | solution.py:54
  76.9 0.7 multiply_convert_fusion.1
  77.7 4.1 %collective-permute-start.4 = (bf16[8,1,768]{2,1,0:T(2,128)(2,1)S(1)}, bf16[8,1,768]{2,1,0:T(2,128)(2,1)S(1)}, u32[]{:S(2)}, u32[]{:S(2)}) collective-permute-start(bf16[8,1,768]{2,1,0:T(2,128)(2,1)S(1)} %get-tuple-element.27), channel_id=1, source_target_pairs={{0,4},{4,8},{8,12},{12,16},{16,20},{20,24},{24,28},{1,5},{5,9},{9,... | collective-permute-start | bytes 36872 | tf_op jit(solution)/shard_map/ppermute | solution.py:17
  81.7 1.3 collective-permute-start.5
  83.0 0.1 multiply_convert_fusion
  83.2 4.2 %collective-permute-done.5 = bf16[8,1,768]{2,1,0:T(2,128)(2,1)S(1)} collective-permute-done((bf16[8,1,768]{2,1,0:T(2,128)(2,1)S(1)}, bf16[8,1,768]{2,1,0:T(2,128)(2,1)S(1)}, u32[]{:S(2)}, u32[]{:S(2)}) %collective-permute-start.5) | collective-permute-done | bytes 12320 | tf_op jit(solution)/shard_map/ppermute | solution.py:19
  87.5 2.8 collective-permute-start.6
  90.3 1.5 collective-permute-start.7
  91.8 3.5 %fusion.2 = f32[3,3,3,96,96]{4,3,2,1,0:T(8,128)S(1)} fusion(bf16[96,10,10,10,1]{0,3,4,2,1:T(8,128)(2,1)S(1)} %get-tuple-element.13, bf16[8,8,8,1,96]{4,2,1,0,3:T(8,128)(2,1)S(1)} %multiply_convert_fusion), kind=kOutput, calls=%fused_computation.10 | convolution fusion | flops 254803968 | bytes 1285632 | tf_op jit(solution)/shard_map/transpose | solution.py:78
  95.3 1.4 copy.49
  96.8 0.3 reshape.254
  97.3 0.4 copy-done.8
  97.6 4.8 %fusion = f32[3,3,3,96,128]{4,3,2,1,0:T(8,128)} fusion(bf16[96,10,10,10,1]{0,3,4,2,1:T(8,128)(2,1)S(1)} %get-tuple-element.11, pred[8,8,8]{2,1,0:T(8,128)(4,1)S(1)} %broadcast_compare_fusion, bf16[8,8,8,1,128]{4,1,2,0,3:T(8,128)(2,1)S(1)} %bitcast.72), kind=kOutput, calls=%fused_computation.8 | convolution fusion | flops 339804160 | bytes 1650688 | tf_op jit(solution)/shard_map/transpose | solution.py:78
  102.5 0.6 copy-done.10
  103.4 3.2 %collective-permute-start.12 = (bf16[8,1,768]{2,1,0:T(2,128)(2,1)S(1)}, bf16[8,1,768]{2,1,0:T(2,128)(2,1)S(1)}, u32[]{:S(2)}, u32[]{:S(2)}) collective-permute-start(bf16[8,1,768]{2,1,0:T(2,128)(2,1)S(1)} %get-tuple-element.25), channel_id=1, source_target_pairs={{0,4},{4,8},{8,12},{12,16},{16,20},{20,24},{24,28},{1,5},{5,9},{9,... | collective-permute-start | bytes 36872 | tf_op jit(solution)/shard_map/ppermute | solution.py:17
  106.6 1.3 collective-permute-start.13
  107.9 54.3 %all-reduce.12.cloned.1.call-done = (f32[2592,96]{0,1:T(8,128)}, f32[2592,128]{1,0:T(8,128)}) async-done(((f32[2592,96]{0,1:T(8,128)}, f32[2592,128]{1,0:T(8,128)}), (f32[2592,96]{0,1:T(8,128)}, f32[2592,128]{1,0:T(8,128)})) %all-reduce.12.cloned.1.call-update) | async-done | bytes 2322448 | tf_op jit(solution)/shard_map/psum | solution.py:143
  162.3 1.5 collective-permute-start.14
  163.9 1.6 collective-permute-start.15
  165.5 2.3 gather_fusion.1
  168.0 0.3 reshape.257
  168.4 5.5 %fusion.4 = f32[1,8,8,8,96]{4,0,3,2,1:T(1,128)S(1)} fusion(bf16[3,3,3,96,96]{4,3,2,1,0:T(8,128)(2,1)S(1)} %bitcast.67, bf16[1,10,10,10,96]{4,3,2,1,0:T(8,128)(2,1)S(1)} %pad_bitcast_fusion.4), kind=kOutput, calls=%fused_computation.12 | convolution fusion | flops 254803968 | bytes 886272 | tf_op jit(solution)/shard_map/conv_general_dilated | solution.py:54
  174.0 1.0 gather_fusion
  175.0 0.8 broadcast_divide_fusion
  175.9 5.5 %all-to-all-start.2 = ((f32[8,64,96]{2,1,0:T(8,128)}), f32[8,64,96]{2,1,0:T(8,128)S(1)}, u32[]{:S(2)}, u32[]{:S(2)}) async-start(f32[8,64,96]{2,1,0:T(8,128)} %broadcast_divide_fusion), calls=%async_computation.2 | async-start | bytes 524288 | tf_op jit(solution)/shard_map/all_to_all | solution.py:148
  181.4 3.4 %convolution_reduce_fusion = f32[8,8,8,128]{3,2,1,0:T(8,128)S(1)} fusion(bf16[3,3,3,96,128]{4,3,2,1,0:T(8,128)(2,1)S(1)} %bitcast.60, bf16[1,10,10,10,96]{4,3,2,1,0:T(8,128)(2,1)S(1)} %get-tuple-element.12), kind=kOutput, calls=%fused_computation.4 | convolution fusion | flops 339738624 | bytes 1117696 | tf_op jit(solution)/shard_map/conv_general_dilated | solution.py:54
  184.9 0.8 fusion.14
  185.7 13.5 %all-to-all-done.2 = f32[8,64,96]{2,1,0:T(8,128)S(1)} async-done(((f32[8,64,96]{2,1,0:T(8,128)}), f32[8,64,96]{2,1,0:T(8,128)S(1)}, u32[]{:S(2)}, u32[]{:S(2)}) %all-to-all-start.2) | async-done | bytes 196640 | tf_op jit(solution)/shard_map/all_to_all | solution.py:148
  199.3 0.3 convolution_bitcast_fusion
  199.6 0.6 slice.119
  200.2 0.6 slice_reduce_fusion
  200.9 79.3 %all-reduce.10.cloned.1.call-done = (f32[2592,96]{0,1:T(8,128)}, f32[2592,128]{1,0:T(8,128)}) async-done(((f32[2592,96]{0,1:T(8,128)}, f32[2592,128]{1,0:T(8,128)}), (f32[2592,96]{0,1:T(8,128)}, f32[2592,128]{1,0:T(8,128)})) %all-reduce.10.cloned.1.call-update) | async-done | bytes 2322448 | tf_op jit(solution)/shard_map/psum | solution.py:142
  280.1 2.3 copy.79
  282.5 1.1 copy.80
  (83 shorter events, 3.1 us)
Async XLA Ops:
  7.2 60.2 %copy-start = (bf16[2592,128]{1,0:T(8,128)(2,1)S(1)}, bf16[2592,128]{1,0:T(8,128)(2,1)}, u32[]{:S(2)}) copy-start(bf16[2592,128]{1,0:T(8,128)(2,1)} %param.20) | copy-start | bytes 1990660
  7.2 35.6 %copy-start.7 = (bf16[2592,96]{0,1:T(8,128)(2,1)S(1)}, bf16[2592,96]{0,1:T(8,128)(2,1)}, u32[]{:S(2)}) copy-start(bf16[2592,96]{0,1:T(8,128)(2,1)} %param.19) | copy-start | bytes 1492996
  9.4 13.7 %all-to-all-start = ((s32[8,1,64]{2,1,0:T(1,128)}), s32[8,1,64]{2,1,0:T(1,128)S(1)}, u32[]{:S(2)}, u32[]{:S(2)}) async-start(s32[8,1,64]{2,1,0:T(1,128)} %compare_select_fusion), calls=%async_computation | async-start | bytes 8192 | tf_op jit(solution)/shard_map/all_to_all | solution.py:117
  23.1 5.5 %copy-start.9 = (s32[8,1,64]{2,1,0:T(1,128)}, s32[8,1,64]{2,1,0:T(1,128)S(1)}, u32[]{:S(2)}) copy-start(s32[8,1,64]{2,1,0:T(1,128)S(1)} %all-to-all-done) | copy-start | bytes 6148
  28.6 54.5 %copy-start.3 = (f32[8,8,8]{2,1,0:T(8,128)}, f32[8,8,8]{2,1,0:T(8,128)S(1)}, u32[]{:S(2)}) copy-start(f32[8,8,8]{2,1,0:T(8,128)S(1)} %reshape.262) | copy-start | bytes 6148
  29.8 13.3 %collective-permute-start.8 = (bf16[8,1,1024]{2,1,0:T(2,128)(2,1)S(1)}, bf16[8,1,1024]{2,1,0:T(2,128)(2,1)S(1)}, u32[]{:S(2)}, u32[]{:S(2)}) collective-permute-start(bf16[8,1,1024]{2,1,0:T(2,128)(2,1)S(1)} %get-tuple-element.23), channel_id=1, source_target_pairs={{0,4},{4,8},{8,12},{12,16},{16,20},{20,24},{24,28},{1,5},{5,9},{9,... | collective-permute-start | bytes 49160 | tf_op jit(solution)/shard_map/ppermute | solution.py:17
  32.2 10.9 %collective-permute-start.9 = (bf16[8,1,1024]{2,1,0:T(2,128)(2,1)S(1)}, bf16[8,1,1024]{2,1,0:T(2,128)(2,1)S(1)}, u32[]{:S(2)}, u32[]{:S(2)}) collective-permute-start(bf16[8,1,1024]{2,1,0:T(2,128)(2,1)S(1)} %get-tuple-element.24), channel_id=1, source_target_pairs={{4,0},{8,4},{12,8},{16,12},{20,16},{24,20},{28,24},{5,1},{9,5},{13... | collective-permute-start | bytes 49160 | tf_op jit(solution)/shard_map/ppermute | solution.py:19
  36.1 14.0 %all-to-all-start.1 = ((bf16[8,64,96]{2,1,0:T(8,128)(2,1)}), bf16[8,64,96]{2,1,0:T(8,128)(2,1)S(1)}, u32[]{:S(2)}, u32[]{:S(2)}) async-start(bf16[8,64,96]{2,1,0:T(8,128)(2,1)} %bitcast.7), calls=%async_computation.1 | async-start | bytes 262144 | tf_op jit(solution)/shard_map/all_to_all | solution.py:116
  42.7 119.5 %all-reduce.12.cloned.1.call-start = ((), (), s32[]{:S(2)}) async-start(), calls=%async_computation.4 | async-start | bytes 4718592 | tf_op jit(solution)/shard_map/psum | solution.py:143
  43.1 29.5 %copy-start.5 = (bf16[2592,96]{1,0:T(8,128)(2,1)}, bf16[2592,96]{1,0:T(8,128)(2,1)S(1)}, u32[]{:S(2)}) copy-start(bf16[2592,96]{1,0:T(8,128)(2,1)S(1)} %copy.40) | copy-start | bytes 1492996
  43.2 2.9 collective-permute-start.10
  44.5 4.8 %collective-permute-start.11 = (bf16[1,10,1024]{2,1,0:T(8,128)(2,1)S(1)}, bf16[1,10,1024]{2,1,0:T(8,128)(2,1)S(1)}, u32[]{:S(2)}, u32[]{:S(2)}) collective-permute-start(bf16[1,10,1024]{2,1,0:T(8,128)(2,1)S(1)} %get-tuple-element.16), channel_id=1, source_target_pairs={{1,0},{2,1},{3,2},{5,4},{6,5},{7,6},{9,8},{10,9},{11,10},{13,12},{... | collective-permute-start | bytes 61448 | tf_op jit(solution)/shard_map/ppermute | solution.py:19
  45.8 7.6 %copy-start.11 = (f32[512]{0:T(512)}, f32[512]{0:T(512)S(1)}, u32[]{:S(2)}) copy-start(f32[512]{0:T(512)S(1)} %maximum_convert_fusion) | copy-start | bytes 6148
  53.6 4.5 %collective-permute-start = (bf16[8,1,768]{2,1,0:T(2,128)(2,1)S(1)}, bf16[8,1,768]{2,1,0:T(2,128)(2,1)S(1)}, u32[]{:S(2)}, u32[]{:S(2)}) collective-permute-start(bf16[8,1,768]{2,1,0:T(2,128)(2,1)S(1)} %get-tuple-element.29), channel_id=1, source_target_pairs={{0,4},{4,8},{8,12},{12,16},{16,20},{20,24},{24,28},{1,5},{5,9},{9,... | collective-permute-start | bytes 36872 | tf_op jit(solution)/shard_map/ppermute | solution.py:17
  56.6 5.9 %collective-permute-start.1 = (bf16[8,1,768]{2,1,0:T(2,128)(2,1)S(1)}, bf16[8,1,768]{2,1,0:T(2,128)(2,1)S(1)}, u32[]{:S(2)}, u32[]{:S(2)}) collective-permute-start(bf16[8,1,768]{2,1,0:T(2,128)(2,1)S(1)} %get-tuple-element.30), channel_id=1, source_target_pairs={{4,0},{8,4},{12,8},{16,12},{20,16},{24,20},{28,24},{5,1},{9,5},{13... | collective-permute-start | bytes 36872 | tf_op jit(solution)/shard_map/ppermute | solution.py:19
  62.6 9.5 %collective-permute-start.2 = (bf16[1,10,768]{2,1,0:T(8,128)(2,1)S(1)}, bf16[1,10,768]{2,1,0:T(8,128)(2,1)S(1)}, u32[]{:S(2)}, u32[]{:S(2)}) collective-permute-start(bf16[1,10,768]{2,1,0:T(8,128)(2,1)S(1)} %get-tuple-element.21), channel_id=1, source_target_pairs={{0,1},{1,2},{2,3},{4,5},{5,6},{6,7},{8,9},{9,10},{10,11},{12,13},{... | collective-permute-start | bytes 46088 | tf_op jit(solution)/shard_map/ppermute | solution.py:17
  65.9 6.2 %collective-permute-start.3 = (bf16[1,10,768]{2,1,0:T(8,128)(2,1)S(1)}, bf16[1,10,768]{2,1,0:T(8,128)(2,1)S(1)}, u32[]{:S(2)}, u32[]{:S(2)}) collective-permute-start(bf16[1,10,768]{2,1,0:T(8,128)(2,1)S(1)} %get-tuple-element.22), channel_id=1, source_target_pairs={{1,0},{2,1},{3,2},{5,4},{6,5},{7,6},{9,8},{10,9},{11,10},{13,12},{... | collective-permute-start | bytes 46088 | tf_op jit(solution)/shard_map/ppermute | solution.py:19
  77.7 5.6 %collective-permute-start.4 = (bf16[8,1,768]{2,1,0:T(2,128)(2,1)S(1)}, bf16[8,1,768]{2,1,0:T(2,128)(2,1)S(1)}, u32[]{:S(2)}, u32[]{:S(2)}) collective-permute-start(bf16[8,1,768]{2,1,0:T(2,128)(2,1)S(1)} %get-tuple-element.27), channel_id=1, source_target_pairs={{0,4},{4,8},{8,12},{12,16},{16,20},{20,24},{24,28},{1,5},{5,9},{9,... | collective-permute-start | bytes 36872 | tf_op jit(solution)/shard_map/ppermute | solution.py:17
  81.7 5.7 %collective-permute-start.5 = (bf16[8,1,768]{2,1,0:T(2,128)(2,1)S(1)}, bf16[8,1,768]{2,1,0:T(2,128)(2,1)S(1)}, u32[]{:S(2)}, u32[]{:S(2)}) collective-permute-start(bf16[8,1,768]{2,1,0:T(2,128)(2,1)S(1)} %get-tuple-element.28), channel_id=1, source_target_pairs={{4,0},{8,4},{12,8},{16,12},{20,16},{24,20},{28,24},{5,1},{9,5},{13... | collective-permute-start | bytes 36872 | tf_op jit(solution)/shard_map/ppermute | solution.py:19
  87.5 9.2 %collective-permute-start.6 = (bf16[1,10,768]{2,1,0:T(8,128)(2,1)S(1)}, bf16[1,10,768]{2,1,0:T(8,128)(2,1)S(1)}, u32[]{:S(2)}, u32[]{:S(2)}) collective-permute-start(bf16[1,10,768]{2,1,0:T(8,128)(2,1)S(1)} %get-tuple-element.19), channel_id=1, source_target_pairs={{0,1},{1,2},{2,3},{4,5},{5,6},{6,7},{8,9},{9,10},{10,11},{12,13},{... | collective-permute-start | bytes 46088 | tf_op jit(solution)/shard_map/ppermute | solution.py:17
  90.3 6.5 %collective-permute-start.7 = (bf16[1,10,768]{2,1,0:T(8,128)(2,1)S(1)}, bf16[1,10,768]{2,1,0:T(8,128)(2,1)S(1)}, u32[]{:S(2)}, u32[]{:S(2)}) collective-permute-start(bf16[1,10,768]{2,1,0:T(8,128)(2,1)S(1)} %get-tuple-element.20), channel_id=1, source_target_pairs={{1,0},{2,1},{3,2},{5,4},{6,5},{7,6},{9,8},{10,9},{11,10},{13,12},{... | collective-permute-start | bytes 46088 | tf_op jit(solution)/shard_map/ppermute | solution.py:19
  96.7 0.9 copy-start.8
  102.5 0.7 copy-start.10
  102.5 0.9 copy-start.2
  102.5 177.6 %all-reduce.10.cloned.1.call-start = ((), (), s32[]{:S(2)}) async-start(), calls=%async_computation.3 | async-start | bytes 4718592 | tf_op jit(solution)/shard_map/psum | solution.py:142
  103.4 62.1 %copy-start.12 = (f32[512]{0:T(512)S(1)}, f32[512]{0:T(512)}, u32[]{:S(2)}) copy-start(f32[512]{0:T(512)} %copy-done.11) | copy-start | bytes 6148
  103.4 62.1 %copy-start.4 = (f32[8,8,8]{2,1,0:T(8,128)S(1)}, f32[8,8,8]{2,1,0:T(8,128)}, u32[]{:S(2)}) copy-start(f32[8,8,8]{2,1,0:T(8,128)} %copy-done.3) | copy-start | bytes 6148
  103.4 58.9 %collective-permute-start.12 = (bf16[8,1,768]{2,1,0:T(2,128)(2,1)S(1)}, bf16[8,1,768]{2,1,0:T(2,128)(2,1)S(1)}, u32[]{:S(2)}, u32[]{:S(2)}) collective-permute-start(bf16[8,1,768]{2,1,0:T(2,128)(2,1)S(1)} %get-tuple-element.25), channel_id=1, source_target_pairs={{0,4},{4,8},{8,12},{12,16},{16,20},{20,24},{24,28},{1,5},{5,9},{9,... | collective-permute-start | bytes 36872 | tf_op jit(solution)/shard_map/ppermute | solution.py:17
  106.6 55.7 %collective-permute-start.13 = (bf16[8,1,768]{2,1,0:T(2,128)(2,1)S(1)}, bf16[8,1,768]{2,1,0:T(2,128)(2,1)S(1)}, u32[]{:S(2)}, u32[]{:S(2)}) collective-permute-start(bf16[8,1,768]{2,1,0:T(2,128)(2,1)S(1)} %get-tuple-element.26), channel_id=1, source_target_pairs={{4,0},{8,4},{12,8},{16,12},{20,16},{24,20},{28,24},{5,1},{9,5},{13... | collective-permute-start | bytes 36872 | tf_op jit(solution)/shard_map/ppermute | solution.py:19
  162.3 5.5 %collective-permute-start.14 = (bf16[1,10,768]{2,1,0:T(8,128)(2,1)S(1)}, bf16[1,10,768]{2,1,0:T(8,128)(2,1)S(1)}, u32[]{:S(2)}, u32[]{:S(2)}) collective-permute-start(bf16[1,10,768]{2,1,0:T(8,128)(2,1)S(1)} %get-tuple-element.17), channel_id=1, source_target_pairs={{0,1},{1,2},{2,3},{4,5},{5,6},{6,7},{8,9},{9,10},{10,11},{12,13},{... | collective-permute-start | bytes 46088 | tf_op jit(solution)/shard_map/ppermute | solution.py:17
  163.9 4.0 %collective-permute-start.15 = (bf16[1,10,768]{2,1,0:T(8,128)(2,1)S(1)}, bf16[1,10,768]{2,1,0:T(8,128)(2,1)S(1)}, u32[]{:S(2)}, u32[]{:S(2)}) collective-permute-start(bf16[1,10,768]{2,1,0:T(8,128)(2,1)S(1)} %get-tuple-element.18), channel_id=1, source_target_pairs={{1,0},{2,1},{3,2},{5,4},{6,5},{7,6},{9,8},{10,9},{11,10},{13,12},{... | collective-permute-start | bytes 46088 | tf_op jit(solution)/shard_map/ppermute | solution.py:19
  165.5 2.9 copy-start.6
  175.9 23.3 %all-to-all-start.2 = ((f32[8,64,96]{2,1,0:T(8,128)}), f32[8,64,96]{2,1,0:T(8,128)S(1)}, u32[]{:S(2)}, u32[]{:S(2)}) async-start(f32[8,64,96]{2,1,0:T(8,128)} %broadcast_divide_fusion), calls=%async_computation.2 | async-start | bytes 524288 | tf_op jit(solution)/shard_map/all_to_all | solution.py:148
  184.8 14.5 %copy-start.13 = (f32[8,96]{1,0:T(8,128)S(1)}, f32[8,96]{1,0:T(8,128)}, u32[]{:S(2)}) copy-start(f32[8,96]{1,0:T(8,128)} %param.17) | copy-start | bytes 9220
  184.8 14.5 %copy-start.14 = (f32[512,96]{0,1:T(8,128)S(1)}, f32[512,96]{0,1:T(8,128)}, u32[]{:S(2)}) copy-start(f32[512,96]{0,1:T(8,128)} %get-tuple-element.38) | copy-start | bytes 589828
  280.1 2.4 copy-start.1
Sparse Core Ops, SparseCore 0:
  102.6 59.6 all-reduce.11
  165.8 114.2 all-reduce.9
